TPU v7x, 512 devices: a whole 4x4x16 slice. The times are simulated.
512 devices in a mesh: rows: 128 (over z, x, core), grp: 4 (over y).
Axes of the slice: x: 4, y: 4, z: 16, core: 2. Of those that a mesh axis runs over, the one named last changes fastest.
Arguments:
- features: bfloat16 [4, 196608, 128], P('grp', 'rows'), may hold values from -6 to 6
- length_scale: bfloat16 [4, 196608], P('grp', 'rows'), may hold values from 32 to 256
- prior: bfloat16 [4, 196608], P('grp', 'rows'), may hold values from 0.45 to 18
- partners: int32 [4, 1536, 16], P('grp', 'rows'), may hold values from 0 to 1535, as said below
- counts: int32 [4, 1536], P('grp', 'rows'), may hold values from 12 to 16
- projection: bfloat16 [128, 64], replicated, may hold values from -0.5 to 0.5
Outputs:
- first_basis: float32 [4, 64, 196608], P('grp', None, 'rows')
- embedding: float32 [4, 64, 196608], P('grp', None, 'rows')
Inputs may be any that keep to these rules, and one draw needn't show every extreme that they name: `partners`: slot 0 of each tile names the tile itself; slots 1 to 12 name tiles held by the same device; slots 13 onward name tiles held by other devices along rows in the same group. Tiles may repeat in a list. Over one device's tiles, slots 13 onward name tiles of any one other device at most 1 times, and exactly 1 times for some device.
All inputs are finite; a program needn't handle non-finite values.
Results may differ from a plain program's by a relative error of at most 0.0047.
Values may be sent and summed in bfloat16 or wider, within the bound.
A program may use at most 128 MiB of HBM per device.

v0:
```python
import jax
import jax.numpy as jnp
from jax import lax
from jax.sharding import PartitionSpec as P

NEAR = 13


def kernel_tiles(own_rows, own_norm, own_band, part_rows, part_norm, part_band, alive_mask):
    cross_products = jnp.einsum(
        "naf,nsbf->nsab", own_rows, part_rows, preferred_element_type=jnp.float32
    )
    distance = jnp.maximum(
        own_norm[:, None, :, None] + part_norm[:, :, None, :] - 2.0 * cross_products, 0.0
    )
    spread = (
        own_band.astype(jnp.float32)[:, None, :, None]
        + part_band.astype(jnp.float32)[:, :, None, :]
    )
    return jnp.where(alive_mask[:, :, None, None], jnp.exp(-distance / spread), 0.0)


def density_term(kernel, extras):
    return jnp.sum(kernel, axis=(1, 3))


def walk_term(kernel, extras):
    rounded = lax.optimization_barrier(kernel.astype(jnp.bfloat16))
    degree = jnp.sum(rounded.astype(jnp.float32) * extras[0][:, :, None, :], axis=(1, 3))
    product = jnp.einsum("nsab,nscb->nca", rounded, extras[1], preferred_element_type=jnp.float32)
    return (degree, product)


def apply_term(kernel, extras):
    rounded = kernel.astype(jnp.bfloat16)
    return jnp.einsum("nsab,nscb->nca", rounded, extras[0], preferred_element_type=jnp.float32)


def sweep_blocks(block_term, own_arrays, pool_arrays, slot_table, alive_table, block_size):
    tiles_dev = own_arrays[0].shape[0]

    def one_block(block_step):
        first_tile = block_step * block_size
        own_block = [
            lax.dynamic_slice_in_dim(member, first_tile, block_size, 0) for member in own_arrays
        ]
        slot_block = lax.dynamic_slice_in_dim(slot_table, first_tile, block_size, 0)
        alive_block = lax.dynamic_slice_in_dim(alive_table, first_tile, block_size, 0)
        gathered = [jnp.take(member, slot_block, axis=0) for member in pool_arrays]
        kernel = kernel_tiles(
            own_block[0],
            own_block[1],
            own_block[2],
            gathered[0],
            gathered[1],
            gathered[2],
            alive_block,
        )
        return block_term(kernel, gathered[3:])

    stacked = lax.map(one_block, jnp.arange(tiles_dev // block_size, dtype=jnp.int32))
    return jax.tree.map(
        lambda stacked_part: stacked_part.reshape((tiles_dev,) + stacked_part.shape[2:]), stacked
    )


def combined(
    block_term,
    own_arrays,
    near_extras,
    far_arrays,
    far_extras,
    near_table,
    far_table,
    alive_table,
    block_size,
):
    pool_arrays = tuple(
        (
            jnp.concatenate([near_member, far_member], axis=0)
            for near_member, far_member in zip(own_arrays + near_extras, far_arrays + far_extras)
        )
    )
    slot_table = jnp.concatenate([near_table, far_table + own_arrays[0].shape[0]], axis=1)
    return sweep_blocks(block_term, own_arrays, pool_arrays, slot_table, alive_table, block_size)


def orthonormal(raw_basis, total_rows):
    local_gram = jnp.einsum("nca,nda->cd", raw_basis, raw_basis, precision=lax.Precision.HIGHEST)
    gram_matrix = lax.psum(local_gram, ("rows", "grp")) / total_rows
    lower = jnp.linalg.cholesky(gram_matrix)
    identity = jnp.eye(gram_matrix.shape[0], dtype=jnp.float32)
    lower_inverse = lax.linalg.triangular_solve(lower, identity, left_side=True, lower=True)
    return jnp.einsum("dc,nca->nda", lower_inverse, raw_basis, precision=lax.Precision.HIGHEST)


def columns_first(tile_basis):
    return jnp.transpose(tile_basis, (1, 0, 2)).reshape(
        1, tile_basis.shape[1], tile_basis.shape[0] * tile_basis.shape[2]
    )


def shards(features, length_scale, prior, partners, counts, projection):
    tiles_dev = partners.shape[1]
    part_slots = partners.shape[2]
    tile_rows = features.shape[1] // tiles_dev
    feature_width = features.shape[2]
    column_count = projection.shape[1]
    nrows = lax.axis_size("rows")
    device_index = lax.axis_index("rows")
    own_rows = features[0].reshape(tiles_dev, tile_rows, feature_width)
    own_band = length_scale[0].reshape(tiles_dev, tile_rows)
    own_prior = prior[0].reshape(tiles_dev, tile_rows)
    own_norm = jnp.einsum("naf,naf->na", own_rows, own_rows, preferred_element_type=jnp.float32)
    partner_lists = partners[0]
    far_tiles = partner_lists[:, NEAR:].reshape(-1)
    far_count = far_tiles.shape[0]
    capacity = max(1, (3 * far_count + 2 * nrows - 3) // (2 * (nrows - 1)))
    near_table = partner_lists[:, :NEAR] - device_index * tiles_dev
    alive_table = jnp.arange(part_slots, dtype=jnp.int32)[None, :] < counts[0][:, None]
    block_size = 2
    owner_index = far_tiles // tiles_dev
    local_index = far_tiles % tiles_dev
    owner_hits = (owner_index[:, None] == jnp.arange(nrows, dtype=jnp.int32)[None, :]).astype(
        jnp.int32
    )
    slot_rank = jnp.sum((jnp.cumsum(owner_hits, axis=0) - owner_hits) * owner_hits, axis=1)
    wanted = jnp.zeros((nrows, capacity), jnp.int32).at[owner_index, slot_rank].set(local_index)
    requested = lax.all_to_all(wanted, "rows", split_axis=0, concat_axis=0, tiled=True)
    got_rows, got_band, got_prior = (
        lax.all_to_all(
            jnp.take(own_rows, requested, axis=0), "rows", split_axis=0, concat_axis=0, tiled=True
        ),
        lax.all_to_all(
            jnp.take(own_band, requested, axis=0), "rows", split_axis=0, concat_axis=0, tiled=True
        ),
        lax.all_to_all(
            jnp.take(own_prior, requested, axis=0), "rows", split_axis=0, concat_axis=0, tiled=True
        ),
    )
    far_rows = got_rows.reshape(nrows * capacity, tile_rows, feature_width)
    far_band = got_band.reshape(nrows * capacity, tile_rows)
    far_prior = got_prior.reshape(nrows * capacity, tile_rows)
    far_table = (owner_index * capacity + slot_rank).reshape(tiles_dev, part_slots - NEAR)
    far_norm = jnp.einsum("naf,naf->na", far_rows, far_rows, preferred_element_type=jnp.float32)
    own_arrays = (own_rows, own_norm, own_band)
    far_arrays = (far_rows, far_norm, far_band)
    density = combined(
        density_term, own_arrays, (), far_arrays, (), near_table, far_table, alive_table, block_size
    )
    own_inverse = 1.0 / density
    far_inverse = (
        lax.all_to_all(
            jnp.take(own_inverse, requested, axis=0).astype(jnp.bfloat16),
            "rows",
            split_axis=0,
            concat_axis=0,
            tiled=True,
        )
        .astype(jnp.float32)
        .reshape(nrows * capacity, tile_rows)
    )
    own_start = jnp.einsum("naf,fc->nca", own_rows, projection, preferred_element_type=jnp.float32)
    own_scaled = (own_start * (own_prior.astype(jnp.float32) * own_inverse)[:, None, :]).astype(
        jnp.bfloat16
    )
    far_start = jnp.einsum("naf,fc->nca", far_rows, projection, preferred_element_type=jnp.float32)
    far_scaled = (far_start * (far_prior.astype(jnp.float32) * far_inverse)[:, None, :]).astype(
        jnp.bfloat16
    )
    degree, product = combined(
        walk_term,
        own_arrays,
        (own_inverse, own_scaled),
        far_arrays,
        (far_inverse, far_scaled),
        near_table,
        far_table,
        alive_table,
        block_size,
    )
    total_rows = nrows * lax.axis_size("grp") * tiles_dev * tile_rows
    first_basis = orthonormal(product / degree[:, None, :], total_rows)
    own_next = (first_basis * own_inverse[:, None, :]).astype(jnp.bfloat16)
    far_next = lax.all_to_all(
        jnp.take(own_next, requested, axis=0), "rows", split_axis=0, concat_axis=0, tiled=True
    ).reshape(nrows * capacity, column_count, tile_rows)
    second = combined(
        apply_term,
        own_arrays,
        (own_next,),
        far_arrays,
        (far_next,),
        near_table,
        far_table,
        alive_table,
        block_size,
    )
    final_basis = orthonormal(second / degree[:, None, :], total_rows)
    return (columns_first(first_basis), columns_first(final_basis))


def solution(mesh):
    in_specs = (
        P("grp", "rows", None),
        P("grp", "rows"),
        P("grp", "rows"),
        P("grp", "rows", None),
        P("grp", "rows"),
        P(),
    )
    out_specs = (P("grp", None, "rows"), P("grp", None, "rows"))
    return jax.shard_map(shards, mesh=mesh, in_specs=in_specs, out_specs=out_specs, check_vma=False)
```

profile of v0, /device:TPU:1, one launch (start us, length us, event | category | flops | bytes accessed | tf_op | source)
XLA Modules:
  0.0 839.4 jit_solution(2037871099502354747)
XLA Ops:
  4.0 20.4 %all-to-all-start = ((s32[128,1,1]{2,1,0:T(1,128)}), s32[128,1,1]{2,1,0:T(1,128)S(1)}, u32[]{:S(2)}, u32[]{:S(2)}) async-start(s32[128,1,1]{2,1,0:T(1,128)} %copy.68), calls=%async_computation | async-start | bytes 131072 | tf_op jit(solution)/shard_map/all_to_all | solution.py:129
  25.8 13.4 %all-to-all-done = s32[128,1,1]{2,1,0:T(1,128)S(1)} async-done(((s32[128,1,1]{2,1,0:T(1,128)}), s32[128,1,1]{2,1,0:T(1,128)S(1)}, u32[]{:S(2)}, u32[]{:S(2)}) %all-to-all-start) | async-done | bytes 544 | tf_op jit(solution)/shard_map/all_to_all | solution.py:129
  48.5 5.6 all-to-all-start.2
  57.2 4.6 fusion.70
  61.7 7.5 all-to-all-done.2
  69.2 9.3 %all-to-all-start.1 = ((bf16[128,1,128,128]{3,2,1,0:T(8,128)(2,1)}), bf16[128,1,128,128]{3,2,1,0:T(8,128)(2,1)}, u32[]{:S(2)}, u32[]{:S(2)}) async-start(bf16[128,1,128,128]{3,2,1,0:T(8,128)(2,1)} %fusion.70), calls=%async_computation.1 | async-start | bytes 8388608 | tf_op jit(solution)/shard_map/all_to_all | solution.py:131
  79.7 182.3 %all-to-all-done.1 = bf16[128,1,128,128]{3,2,1,0:T(8,128)(2,1)} async-done(((bf16[128,1,128,128]{3,2,1,0:T(8,128)(2,1)}), bf16[128,1,128,128]{3,2,1,0:T(8,128)(2,1)}, u32[]{:S(2)}, u32[]{:S(2)}) %all-to-all-start.1) | async-done | bytes 4194336 | tf_op jit(solution)/shard_map/all_to_all | solution.py:131
  262.1 4.6 pad_maximum_fusion
  266.7 4.4 fusion.69
  271.2 45.2 %while.32 = (s32[]{:T(128)}, f32[6,2,128]{2,1,0:T(2,128)S(1)}, s32[6]{0:T(128)S(1)}, pred[12,16]{1,0:T(8,128)(4,1)S(1)}, f32[12,128]{1,0:T(8,128)S(1)}, /*index=...) while((s32[]{:T(128)}, f32[6,2,128]{2,1,0:T(2,128)S(1)}, ...), condition=%wide.region_5.10_spmd, body=%wide.region_3.9_spmd.sunk | while | flops 139474112 | bytes 3365755 | solution.py:61
  273.8 3.0 gather_fusion
  281.3 3.0 gather_fusion
  288.8 3.0 gather_fusion
  296.4 3.0 gather_fusion
  311.4 3.0 gather_fusion
  317.8 13.1 %all-to-all-start.3 = ((bf16[128,1,128]{2,1,0:T(2,128)(2,1)}), bf16[128,1,128]{2,1,0:T(2,128)(2,1)S(1)}, u32[]{:S(2)}, u32[]{:S(2)}) async-start(bf16[128,1,128]{2,1,0:T(2,128)(2,1)} %copy.71), calls=%async_computation.3 | async-start | bytes 131072 | tf_op jit(solution)/shard_map/all_to_all | solution.py:153
  330.9 14.8 %all-to-all-done.3 = bf16[128,1,128]{2,1,0:T(2,128)(2,1)S(1)} async-done(((bf16[128,1,128]{2,1,0:T(2,128)(2,1)}), bf16[128,1,128]{2,1,0:T(2,128)(2,1)S(1)}, u32[]{:S(2)}, u32[]{:S(2)}) %all-to-all-start.3) | async-done | bytes 32800 | tf_op jit(solution)/shard_map/all_to_all | solution.py:153
  345.7 5.9 all-to-all-start.4
  352.1 14.5 %all-to-all-done.4 = bf16[128,1,128]{2,1,0:T(2,128)(2,1)S(1)} async-done(((bf16[128,1,128]{2,1,0:T(2,128)(2,1)}), bf16[128,1,128]{2,1,0:T(2,128)(2,1)S(1)}, u32[]{:S(2)}, u32[]{:S(2)}) %all-to-all-start.4) | async-done | bytes 32800 | tf_op jit(solution)/shard_map/all_to_all | solution.py:137
  366.6 3.8 fusion.72
  372.1 69.3 %while.33 = (s32[]{:T(128)}, f32[6,2,128]{2,1,0:T(2,128)S(1)}, f32[6,2,64,128]{3,2,1,0:T(8,128)S(1)}, s32[6]{0:T(128)S(1)}, pred[12,16]{1,0:T(8,128)(4,1)S(1)}, ...) while((s32[]{:T(128)}, f32[6,2,128]{2,1,0:T(2,128)S(1)}, ...), condition=%wide.region_8.14_spmd, body=%wide.region_6.13_spmd.sunk | while | flops 208422080 | bytes 8232599 | solution.py:61
  386.9 3.0 gather_fusion.3
  398.4 3.0 gather_fusion.3
  441.9 100.7 %psum.14 = f32[64,64]{0,1:T(8,128)S(1)} all-reduce(f32[64,64]{0,1:T(8,128)S(1)} %convolution_bitcast_fusion.4), channel_id=1, replica_groups=mesh['rows'=128,'grp'=4] {'rows','grp'}, use_global_device_ids=true, to_apply=%region_9.15 | all-reduce | flops 4096 | bytes 32768 | tf_op jit(solution)/shard_map/psum | solution.py:90
  542.7 5.8 cholesky.44
  549.9 4.9 custom-call.6
  558.1 9.4 %all-to-all-start.5 = ((bf16[128,1,64,128]{3,2,1,0:T(8,128)(2,1)}), bf16[128,1,64,128]{3,2,1,0:T(8,128)(2,1)S(1)}, u32[]{:S(2)}, u32[]{:S(2)}) async-start(bf16[128,1,64,128]{3,2,1,0:T(8,128)(2,1)} %fusion.71), calls=%async_computation.5 | async-start | bytes 4194304 | tf_op jit(solution)/shard_map/all_to_all | solution.py:185
  570.5 93.9 %all-to-all-done.5 = bf16[128,1,64,128]{3,2,1,0:T(8,128)(2,1)S(1)} async-done(((bf16[128,1,64,128]{3,2,1,0:T(8,128)(2,1)}), bf16[128,1,64,128]{3,2,1,0:T(8,128)(2,1)S(1)}, u32[]{:S(2)}, u32[]{:S(2)}) %all-to-all-start.5) | async-done | bytes 2097184 | tf_op jit(solution)/shard_map/all_to_all | solution.py:185
  666.0 57.1 %while.34 = (s32[]{:T(128)}, f32[6,2,64,128]{3,2,1,0:T(8,128)S(1)}, s32[6]{0:T(128)S(1)}, s32[12,16]{1,0:T(8,128)S(1)}, bf16[140,64,128]{2,1,0:T(8,128)(2,1)}, /...) while((s32[]{:T(128)}, f32[6,2,64,128]{3,2,1,0:T(8,128)S(1)}, ...), condition=%wide.region_13.21_spmd, body=%wide.region_12.20_spmd.sunk | while | flops 206845376 | bytes 5001731 | solution.py:61
  723.6 101.9 %psum.15 = f32[64,64]{0,1:T(8,128)S(1)} all-reduce(f32[64,64]{0,1:T(8,128)S(1)} %convolution_bitcast_fusion.2), channel_id=1, replica_groups=mesh['rows'=128,'grp'=4] {'rows','grp'}, use_global_device_ids=true, to_apply=%region_14.22 | all-reduce | flops 4096 | bytes 32768 | tf_op jit(solution)/shard_map/psum | solution.py:90
  825.6 5.8 cholesky.55
  832.8 4.9 custom-call.7
  (341 shorter events, 173.3 us)
Async XLA Ops:
  0.6 351.1 %copy-start = (bf16[128,64]{0,1:T(8,128)(2,1)S(1)}, bf16[128,64]{0,1:T(8,128)(2,1)}, u32[]{:S(2)}) copy-start(bf16[128,64]{0,1:T(8,128)(2,1)} %param.30) | copy-start | bytes 49156
  0.6 53.5 %copy-start.1 = (bf16[1,1536,128]{2,1,0:T(8,128)(2,1)S(1)}, bf16[1,1536,128]{2,1,0:T(8,128)(2,1)}, u32[]{:S(2)}) copy-start(bf16[1,1536,128]{2,1,0:T(8,128)(2,1)} %param.25) | copy-start | bytes 1179652
  4.0 35.2 %all-to-all-start = ((s32[128,1,1]{2,1,0:T(1,128)}), s32[128,1,1]{2,1,0:T(1,128)S(1)}, u32[]{:S(2)}, u32[]{:S(2)}) async-start(s32[128,1,1]{2,1,0:T(1,128)} %copy.68), calls=%async_computation | async-start | bytes 131072 | tf_op jit(solution)/shard_map/all_to_all | solution.py:129
  48.5 20.7 %all-to-all-start.2 = ((bf16[128,1,128]{2,1,0:T(2,128)(2,1)}), bf16[128,1,128]{2,1,0:T(2,128)(2,1)S(1)}, u32[]{:S(2)}, u32[]{:S(2)}) async-start(bf16[128,1,128]{2,1,0:T(2,128)(2,1)} %copy.70), calls=%async_computation.2 | async-start | bytes 131072 | tf_op jit(solution)/shard_map/all_to_all | solution.py:134
  61.7 17.2 %copy-start.2 = (s32[1,12]{1,0:T(1,128)S(1)}, s32[1,12]{1,0:T(1,128)}, u32[]{:S(2)}) copy-start(s32[1,12]{1,0:T(1,128)} %param.29) | copy-start | bytes 148
  69.2 192.9 %all-to-all-start.1 = ((bf16[128,1,128,128]{3,2,1,0:T(8,128)(2,1)}), bf16[128,1,128,128]{3,2,1,0:T(8,128)(2,1)}, u32[]{:S(2)}, u32[]{:S(2)}) async-start(bf16[128,1,128,128]{3,2,1,0:T(8,128)(2,1)} %fusion.70), calls=%async_computation.1 | async-start | bytes 8388608 | tf_op jit(solution)/shard_map/all_to_all | solution.py:131
  317.8 28.0 %all-to-all-start.3 = ((bf16[128,1,128]{2,1,0:T(2,128)(2,1)}), bf16[128,1,128]{2,1,0:T(2,128)(2,1)S(1)}, u32[]{:S(2)}, u32[]{:S(2)}) async-start(bf16[128,1,128]{2,1,0:T(2,128)(2,1)} %copy.71), calls=%async_computation.3 | async-start | bytes 131072 | tf_op jit(solution)/shard_map/all_to_all | solution.py:153
  345.7 20.8 %all-to-all-start.4 = ((bf16[128,1,128]{2,1,0:T(2,128)(2,1)}), bf16[128,1,128]{2,1,0:T(2,128)(2,1)S(1)}, u32[]{:S(2)}, u32[]{:S(2)}) async-start(bf16[128,1,128]{2,1,0:T(2,128)(2,1)} %copy.72), calls=%async_computation.4 | async-start | bytes 131072 | tf_op jit(solution)/shard_map/all_to_all | solution.py:137
  558.1 106.2 %all-to-all-start.5 = ((bf16[128,1,64,128]{3,2,1,0:T(8,128)(2,1)}), bf16[128,1,64,128]{3,2,1,0:T(8,128)(2,1)S(1)}, u32[]{:S(2)}, u32[]{:S(2)}) async-start(bf16[128,1,64,128]{3,2,1,0:T(8,128)(2,1)} %fusion.71), calls=%async_computation.5 | async-start | bytes 4194304 | tf_op jit(solution)/shard_map/all_to_all | solution.py:185
where the time goes:
time: 850 us; the launch traced here: 839 us
  waiting for transfers between devices  326 us (38%)
  blocking collectives  203 us (24%)
  local copies, waits for them, and re-layouts  133 us (16%)
  starting transfers between devices  63.9 us (8%)
  other arithmetic  60.4 us (7%)
  matrix products  40 us (5%)
  loops' own time  11.9 us (1%)
    psum x2, blocking collectives, orthonormal(): gram_matrix = lax.psum(local_gram, ('rows', 'grp')) / total_rows  203 us
    all_to_all x1, waiting for transfers between devices, shards(): lax.all_to_all(jnp.take(own_rows, requested, axis=0), 'rows', split_axis=...  182 us
    gather x72, local copies, waits for them, and re-layouts, one_block(): gathered = [jnp.take(member, slot_block, axis=0) for member in pool_arrays]  107 us
    all_to_all x1, waiting for transfers between devices, shards(): lax.all_to_all(jnp.take(own_next, requested, axis=0), 'rows', split_axis=...  93.9 us
    dot_general x12, matrix products, kernel_tiles(): jnp.einsum('naf,nsbf->nsab', own_rows, part_rows, preferred_element_type=...  21.5 us
    all_to_all x1, starting transfers between devices, shards(): lax.all_to_all(wanted, 'rows', split_axis=0, concat_axis=0, tiled=True)  20.4 us
  transfers between devices with their start and end apart: 6, of which 6 were waited for; matrix products, arithmetic and copies ran while one was open for 2% of the time, Pallas kernels for 0%

commit v1 on v0

--- a/solution.py
+++ b/solution.py
@@ -87,7 +87,7 @@
 
 def orthonormal(raw_basis, total_rows):
     local_gram = jnp.einsum("nca,nda->cd", raw_basis, raw_basis, precision=lax.Precision.HIGHEST)
-    gram_matrix = lax.psum(local_gram, ("rows", "grp")) / total_rows
+    gram_matrix = jnp.sum(lax.all_gather(local_gram, ("rows", "grp")), axis=0) / total_rows
     lower = jnp.linalg.cholesky(gram_matrix)
     identity = jnp.eye(gram_matrix.shape[0], dtype=jnp.float32)
     lower_inverse = lax.linalg.triangular_solve(lower, identity, left_side=True, lower=True)

time: 850 us -> 1100 us (1.29)
  waiting for transfers between devices: 326 us -> 753 us
  blocking collectives: 203 us -> 0 us
  other arithmetic: 60.4 us -> 74.3 us
  between operations: 1.32 us -> 14.7 us
    all_gather x0 -> x2, waiting for transfers between devices: none -> 424 us  [orthonormal(): lax.all_gather(local_gram, ('rows', 'grp'))]
    psum x2 -> x0, blocking collectives: 203 us -> none  [orthonormal(): gram_matrix = lax.psum(local_gram, ('rows', 'grp')) / total_rows]
    reduce_sum x0 -> x2, other arithmetic: none -> 13.9 us  [orthonormal(): jnp.sum(lax.all_gather(local_gram, ('rows', 'grp')), axis=0) / total_rows]
  transfers between devices with their start and end apart: 6 -> 8, of which waited for: 6 -> 8; matrix products, arithmetic and copies ran while one was open for 2% -> 1% of each run, Pallas kernels for 0% -> 0%
where the time goes in v1:
time: 1100 us; the launch traced here: 1090 us
  waiting for transfers between devices  753 us (68%)
  local copies, waits for them, and re-layouts  132 us (12%)
  other arithmetic  74.3 us (7%)
  starting transfers between devices  66.1 us (6%)
  matrix products  41.1 us (4%)
  between operations  14.7 us (1%)
  loops' own time  12.8 us (1%)
    all_gather x2, waiting for transfers between devices, orthonormal(): lax.all_gather(local_gram, ('rows', 'grp'))  424 us
    all_to_all x1, waiting for transfers between devices, shards(): lax.all_to_all(jnp.take(own_rows, requested, axis=0), 'rows', split_axis=...  182 us
    gather x72, local copies, waits for them, and re-layouts, one_block(): gathered = [jnp.take(member, slot_block, axis=0) for member in pool_arrays]  107 us
    all_to_all x1, waiting for transfers between devices, shards(): lax.all_to_all(jnp.take(own_next, requested, axis=0), 'rows', split_axis=...  96.6 us
  transfers between devices with their start and end apart: 8, of which 8 were waited for; matrix products, arithmetic and copies ran while one was open for 1% of the time, Pallas kernels for 0%

profile of v1, /device:TPU:1, one launch (start us, length us, event | category | flops | bytes accessed | tf_op | source)
XLA Modules:
  0.0 1093.8 jit_solution(13079601982143777893)
XLA Ops:
  10.5 20.4 %all-to-all-start = ((s32[128,1,1]{2,1,0:T(1,128)}), s32[128,1,1]{2,1,0:T(1,128)S(1)}, u32[]{:S(2)}, u32[]{:S(2)}) async-start(s32[128,1,1]{2,1,0:T(1,128)} %copy.64), calls=%async_computation | async-start | bytes 131072 | tf_op jit(solution)/shard_map/all_to_all | solution.py:129
  32.4 13.4 %all-to-all-done = s32[128,1,1]{2,1,0:T(1,128)S(1)} async-done(((s32[128,1,1]{2,1,0:T(1,128)}), s32[128,1,1]{2,1,0:T(1,128)S(1)}, u32[]{:S(2)}, u32[]{:S(2)}) %all-to-all-start) | async-done | bytes 544 | tf_op jit(solution)/shard_map/all_to_all | solution.py:129
  55.0 5.6 all-to-all-start.2
  60.7 3.1 gather_fusion.12
  63.8 4.6 fusion.70
  68.4 7.4 all-to-all-done.2
  75.8 9.9 all-to-all-start.1
  86.8 182.3 %all-to-all-done.1 = bf16[128,1,128,128]{3,2,1,0:T(8,128)(2,1)} async-done(((bf16[128,1,128,128]{3,2,1,0:T(8,128)(2,1)}), bf16[128,1,128,128]{3,2,1,0:T(8,128)(2,1)}, u32[]{:S(2)}, u32[]{:S(2)}) %all-to-all-start.1) | async-done | bytes 4194336 | tf_op jit(solution)/shard_map/all_to_all | solution.py:131
  269.2 4.6 pad_maximum_fusion
  273.8 4.4 fusion.69
  278.3 45.6 %while.32 = (s32[]{:T(128)}, f32[6,2,128]{2,1,0:T(2,128)S(1)}, s32[6]{0:T(128)S(1)}, pred[12,16]{1,0:T(8,128)(4,1)S(1)}, f32[12,128]{1,0:T(8,128)S(1)}, /*index=...) while((s32[]{:T(128)}, f32[6,2,128]{2,1,0:T(2,128)S(1)}, ...), condition=%wide.region_5.10_spmd, body=%wide.region_3.9_spmd.sunk | while | flops 139474112 | bytes 3365755 | solution.py:61
  280.9 3.0 gather_fusion
  303.7 3.0 gather_fusion
  311.3 3.0 gather_fusion
  318.9 3.0 gather_fusion
  325.3 13.1 %all-to-all-start.3 = ((bf16[128,1,128]{2,1,0:T(2,128)(2,1)}), bf16[128,1,128]{2,1,0:T(2,128)(2,1)S(1)}, u32[]{:S(2)}, u32[]{:S(2)}) async-start(bf16[128,1,128]{2,1,0:T(2,128)(2,1)} %copy.67), calls=%async_computation.3 | async-start | bytes 131072 | tf_op jit(solution)/shard_map/all_to_all | solution.py:153
  338.5 14.8 %all-to-all-done.3 = bf16[128,1,128]{2,1,0:T(2,128)(2,1)S(1)} async-done(((bf16[128,1,128]{2,1,0:T(2,128)(2,1)}), bf16[128,1,128]{2,1,0:T(2,128)(2,1)S(1)}, u32[]{:S(2)}, u32[]{:S(2)}) %all-to-all-start.3) | async-done | bytes 32800 | tf_op jit(solution)/shard_map/all_to_all | solution.py:153
  353.3 5.6 all-to-all-start.4
  359.5 14.5 %all-to-all-done.4 = bf16[128,1,128]{2,1,0:T(2,128)(2,1)S(1)} async-done(((bf16[128,1,128]{2,1,0:T(2,128)(2,1)}), bf16[128,1,128]{2,1,0:T(2,128)(2,1)S(1)}, u32[]{:S(2)}, u32[]{:S(2)}) %all-to-all-start.4) | async-done | bytes 32800 | tf_op jit(solution)/shard_map/all_to_all | solution.py:137
  374.1 3.8 fusion.72
  379.5 69.3 %while.33 = (s32[]{:T(128)}, f32[6,2,128]{2,1,0:T(2,128)S(1)}, f32[6,2,64,128]{3,2,1,0:T(8,128)S(1)}, s32[6]{0:T(128)S(1)}, pred[12,16]{1,0:T(8,128)(4,1)S(1)}, ...) while((s32[]{:T(128)}, f32[6,2,128]{2,1,0:T(2,128)S(1)}, ...), condition=%wide.region_8.14_spmd, body=%wide.region_6.13_spmd.sunk | while | flops 208422080 | bytes 8232599 | solution.py:61
  449.9 210.7 %all-gather.5.cloned.1.call-done = f32[32768,64]{1,0:T(8,128)} async-done(((f32[64,64]{1,0:T(8,128)}), f32[32768,64]{1,0:T(8,128)}) %all-gather.5.cloned.1.call-update) | async-done | bytes 8388624 | tf_op jit(solution)/shard_map/all_gather | solution.py:90
  660.6 6.9 reduce_sum.52
  667.8 5.8 cholesky.44
  674.9 4.9 custom-call.6
  683.2 10.9 all-to-all-start.5
  694.4 96.6 %all-to-all-done.5 = bf16[128,1,64,128]{3,2,1,0:T(8,128)(2,1)S(1)} async-done(((bf16[128,1,64,128]{3,2,1,0:T(8,128)(2,1)}), bf16[128,1,64,128]{3,2,1,0:T(8,128)(2,1)S(1)}, u32[]{:S(2)}, u32[]{:S(2)}) %all-to-all-start.5) | async-done | bytes 2097184 | tf_op jit(solution)/shard_map/all_to_all | solution.py:185
  792.6 57.7 %while.34 = (s32[]{:T(128)}, f32[6,2,64,128]{3,2,1,0:T(8,128)S(1)}, s32[6]{0:T(128)S(1)}, s32[12,16]{1,0:T(8,128)S(1)}, bf16[140,64,128]{2,1,0:T(8,128)(2,1)}, /...) while((s32[]{:T(128)}, f32[6,2,64,128]{3,2,1,0:T(8,128)S(1)}, ...), condition=%wide.region_13.21_spmd, body=%wide.region_12.20_spmd.sunk | while | flops 206845376 | bytes 5001731 | solution.py:61
  852.5 213.5 %all-gather.7.cloned.1.call-done = f32[32768,64]{1,0:T(8,128)} async-done(((f32[64,64]{1,0:T(8,128)}), f32[32768,64]{1,0:T(8,128)}) %all-gather.7.cloned.1.call-update) | async-done | bytes 8388624 | tf_op jit(solution)/shard_map/all_gather | solution.py:90
  1066.0 6.9 reduce_sum.53
  1073.1 5.8 cholesky.55
  1080.3 4.9 custom-call.7
  (351 shorter events, 179.5 us)
Async XLA Ops:
  7.2 352.0 %copy-start = (bf16[128,64]{0,1:T(8,128)(2,1)S(1)}, bf16[128,64]{0,1:T(8,128)(2,1)}, u32[]{:S(2)}) copy-start(bf16[128,64]{0,1:T(8,128)(2,1)} %param.30) | copy-start | bytes 49156
  7.2 53.5 %copy-start.2 = (bf16[1,1536,128]{2,1,0:T(8,128)(2,1)S(1)}, bf16[1,1536,128]{2,1,0:T(8,128)(2,1)}, u32[]{:S(2)}) copy-start(bf16[1,1536,128]{2,1,0:T(8,128)(2,1)} %param.25) | copy-start | bytes 1179652
  10.5 35.2 %all-to-all-start = ((s32[128,1,1]{2,1,0:T(1,128)}), s32[128,1,1]{2,1,0:T(1,128)S(1)}, u32[]{:S(2)}, u32[]{:S(2)}) async-start(s32[128,1,1]{2,1,0:T(1,128)} %copy.64), calls=%async_computation | async-start | bytes 131072 | tf_op jit(solution)/shard_map/all_to_all | solution.py:129
  55.0 20.7 %all-to-all-start.2 = ((bf16[128,1,128]{2,1,0:T(2,128)(2,1)}), bf16[128,1,128]{2,1,0:T(2,128)(2,1)S(1)}, u32[]{:S(2)}, u32[]{:S(2)}) async-start(bf16[128,1,128]{2,1,0:T(2,128)(2,1)} %copy.66), calls=%async_computation.2 | async-start | bytes 131072 | tf_op jit(solution)/shard_map/all_to_all | solution.py:134
  68.4 17.7 %copy-start.3 = (s32[1,12]{1,0:T(1,128)S(1)}, s32[1,12]{1,0:T(1,128)}, u32[]{:S(2)}) copy-start(s32[1,12]{1,0:T(1,128)} %param.29) | copy-start | bytes 148
  75.8 193.4 %all-to-all-start.1 = ((bf16[128,1,128,128]{3,2,1,0:T(8,128)(2,1)}), bf16[128,1,128,128]{3,2,1,0:T(8,128)(2,1)}, u32[]{:S(2)}, u32[]{:S(2)}) async-start(bf16[128,1,128,128]{3,2,1,0:T(8,128)(2,1)} %fusion.70), calls=%async_computation.1 | async-start | bytes 8388608 | tf_op jit(solution)/shard_map/all_to_all | solution.py:131
  325.3 28.0 %all-to-all-start.3 = ((bf16[128,1,128]{2,1,0:T(2,128)(2,1)}), bf16[128,1,128]{2,1,0:T(2,128)(2,1)S(1)}, u32[]{:S(2)}, u32[]{:S(2)}) async-start(bf16[128,1,128]{2,1,0:T(2,128)(2,1)} %copy.67), calls=%async_computation.3 | async-start | bytes 131072 | tf_op jit(solution)/shard_map/all_to_all | solution.py:153
  353.3 20.7 %all-to-all-start.4 = ((bf16[128,1,128]{2,1,0:T(2,128)(2,1)}), bf16[128,1,128]{2,1,0:T(2,128)(2,1)S(1)}, u32[]{:S(2)}, u32[]{:S(2)}) async-start(bf16[128,1,128]{2,1,0:T(2,128)(2,1)} %copy.68), calls=%async_computation.4 | async-start | bytes 131072 | tf_op jit(solution)/shard_map/all_to_all | solution.py:137
  358.9 301.7 %all-gather.5.cloned.1.call-start = ((), (), s32[]{:S(2)}) async-start(), calls=%async_computation.6 | async-start | bytes 16809984 | tf_op jit(solution)/shard_map/all_gather | solution.py:90
  683.2 107.8 %all-to-all-start.5 = ((bf16[128,1,64,128]{3,2,1,0:T(8,128)(2,1)}), bf16[128,1,64,128]{3,2,1,0:T(8,128)(2,1)S(1)}, u32[]{:S(2)}, u32[]{:S(2)}) async-start(bf16[128,1,64,128]{3,2,1,0:T(8,128)(2,1)} %fusion.71), calls=%async_computation.5 | async-start | bytes 4194304 | tf_op jit(solution)/shard_map/all_to_all | solution.py:185
  694.1 371.9 %all-gather.7.cloned.1.call-start = ((), (), s32[]{:S(2)}) async-start(), calls=%async_computation.7 | async-start | bytes 16809984 | tf_op jit(solution)/shard_map/all_gather | solution.py:90
  1066.0 20.7 %copy-start.1 = (bf16[128,64]{0,1:T(8,128)(2,1)S(1)}, bf16[128,64]{0,1:T(8,128)(2,1)}, u32[]{:S(2)}) copy-start(bf16[128,64]{0,1:T(8,128)(2,1)} %param.30) | copy-start | bytes 49156
Sparse Core Ops, SparseCore 0:
  450.1 210.5 all-gather.4
  851.6 214.3 all-gather.6
